TPU v7x, 32 devices: a whole 2x2x4 slice. The times are simulated.
32 devices in a mesh: section: 2 (over core), experts: 4 (over z), dp: 4 (over y, x).
Axes of the slice: x: 2, y: 2, z: 4, core: 2. Of those that a mesh axis runs over, the one named last changes fastest.
Arguments:
- tokens: bfloat16 [6304, 768], P(('experts', 'dp')), may hold values from -6 to 6
- cotangent: bfloat16 [6304, 768], P(('experts', 'dp')), may hold values from -6 to 6
- norm_gains: float32 [2, 2, 768], P('section'), may hold values from 0.5 to 1.5
- norm_biases: float32 [2, 2, 768], P('section'), may hold values from -1.5 to 1.5
- qkv_weight: bfloat16 [2, 768, 2304], P('section'), may hold values from -4 to 4
- out_weight: bfloat16 [2, 768, 768], P('section'), may hold values from -1.5 to 1.5
- dense_in: bfloat16 [768, 3072], replicated, may hold values from -0.21875 to 0.21875
- dense_out: bfloat16 [3072, 768], replicated, may hold values from -0.109375 to 0.109375
- expert_in: bfloat16 [4, 768, 3072], P('experts', None, 'dp'), may hold values from -0.21875 to 0.21875
- expert_out: bfloat16 [4, 3072, 768], P('experts', 'dp'), may hold values from -0.109375 to 0.109375
- routes: int32 [6304, 2], P(('experts', 'dp')), may hold values from 0 to 3, all different within a row
- gates: float32 [6304, 2], P(('experts', 'dp')), may hold values from 0.1 to 0.6
Outputs:
- acts: bfloat16 [2, 6304, 768], P('section', ('experts', 'dp'))
- act_grads: float32 [2, 6304, 768], P('section', ('experts', 'dp'))
- qkv_grad: float32 [2, 768, 2304], P('section', ('experts', 'dp'))
- out_grad: float32 [2, 768, 768], P('section', ('experts', 'dp'))
- gain_grad: float32 [2, 2, 768], P('section', None, ('experts', 'dp'))
- bias_grad: float32 [2, 2, 768], P('section', None, ('experts', 'dp'))
- dense_in_grad: float32 [768, 3072], P(('experts', 'dp'), 'section')
- dense_out_grad: float32 [3072, 768], P(('experts', 'dp'), 'section')
- expert_in_grad: float32 [4, 768, 3072], P('experts', 'section', 'dp')
- expert_out_grad: float32 [4, 3072, 768], P('experts', 'dp', 'section')
Inputs may be any that keep to these rules, and one draw needn't show every extreme that they name: `routes`: each row names two different experts, and every expert is named by some row.
All inputs are finite; a program needn't handle non-finite values.
Results may differ from a plain program's by a relative error of at most 0.015.
The roundings to bfloat16 on the way count: a program that leaves them out, or rounds other values in their place, can miss the bound.
Values may be sent and summed in bfloat16 or wider, within the bound.
A program may use at most 448 MiB of HBM per device.

v0:
```python
import jax
import jax.numpy as jnp
from jax import lax
from jax.sharding import PartitionSpec as P

HEADS = 12
HEAD_DIM = 64
SEQ = 197
IMG_MB = 1
MB = 2


eps = 1e-06


def swapped(block, axis, stride):
    count = lax.axis_size(axis)
    route = []
    for low in range(count):
        high = low | 1 << stride
        if high != low and high < count:
            route += [(low, high), (high, low)]
    return lax.ppermute(block, axis, route)


def layer_norm(values, gain, bias):
    centred = values - jnp.mean(values, axis=-1, keepdims=True)
    spread = jnp.mean(centred * centred, axis=-1, keepdims=True)
    return centred * lax.rsqrt(spread + eps) * gain + bias


def norm_back(values, gain, bias, cotan):
    _, pull = jax.vjp(layer_norm, values, gain, bias)
    return pull(cotan)


def gelu_back(before, cotan):
    _, pull = jax.vjp(jax.nn.gelu, before)
    return pull(cotan)[0]


def matmul(left, right):
    return jnp.dot(left, right, preferred_element_type=jnp.float32)


def matmul_rows(left, right):
    return lax.dot_general(
        left, right, (((0,), (0,)), ((), ())), preferred_element_type=jnp.float32
    )


def matmul_cols(left, right):
    return lax.dot_general(
        left, right, (((1,), (1,)), ((), ())), preferred_element_type=jnp.float32
    )


def head_split(mixed):
    return mixed.reshape(-1, SEQ, 3, HEADS, HEAD_DIM)


def score_table(split):
    return jnp.einsum(
        "bqhd,bkhd->bhqk", split[:, :, 0], split[:, :, 1], preferred_element_type=jnp.float32
    ) * HEAD_DIM ** (-0.5)


def attend(normed, weight_qkv):
    mixed = matmul(normed, weight_qkv).astype(jnp.bfloat16)
    split = head_split(mixed)
    scores = score_table(split)
    top = jnp.max(scores, axis=-1, keepdims=True)
    logsum = top + jnp.log(jnp.sum(jnp.exp(scores - top), axis=-1, keepdims=True))
    probs = jnp.exp(scores - logsum).astype(jnp.bfloat16)
    attended = jnp.einsum(
        "bhqk,bkhd->bqhd", probs, split[:, :, 2], preferred_element_type=jnp.float32
    )
    return (mixed, logsum, attended.reshape(normed.shape[0], -1).astype(jnp.bfloat16))


def attend_back(normed, mixed, logsum, attended, grad_hidden, weight_qkv, weight_out):
    grad_cast = grad_hidden.astype(jnp.bfloat16)
    grad_wout = matmul_rows(attended, grad_cast)
    grad_att = matmul_cols(grad_cast, weight_out).astype(jnp.bfloat16)
    split = head_split(mixed)
    probs_full = jnp.exp(score_table(split) - logsum)
    probs = probs_full.astype(jnp.bfloat16)
    grad_heads = grad_att.reshape(-1, SEQ, HEADS, HEAD_DIM)
    grad_probs = jnp.einsum(
        "bqhd,bkhd->bhqk", grad_heads, split[:, :, 2], preferred_element_type=jnp.float32
    )
    grad_value = jnp.einsum(
        "bhqk,bqhd->bkhd", probs, grad_heads, preferred_element_type=jnp.float32
    )
    inner = jnp.sum(probs_full * grad_probs, axis=-1, keepdims=True)
    grad_scores = (probs_full * (grad_probs - inner) * HEAD_DIM ** (-0.5)).astype(jnp.bfloat16)
    grad_query = jnp.einsum(
        "bhqk,bkhd->bqhd", grad_scores, split[:, :, 1], preferred_element_type=jnp.float32
    )
    grad_key = jnp.einsum(
        "bhqk,bqhd->bkhd", grad_scores, split[:, :, 0], preferred_element_type=jnp.float32
    )
    grad_mixed = (
        jnp.stack([grad_query, grad_key, grad_value], axis=2)
        .reshape(normed.shape[0], -1)
        .astype(jnp.bfloat16)
    )
    return (matmul_cols(grad_mixed, weight_qkv), matmul_rows(normed, grad_mixed), grad_wout)


def front_half(block_in, gains, biases, weight_qkv, weight_out):
    start = block_in.astype(jnp.float32)
    normed = layer_norm(start, gains[0], biases[0]).astype(jnp.bfloat16)
    mixed, logsum, attended = attend(normed, weight_qkv)
    hidden = start + matmul(attended, weight_out)
    second = layer_norm(hidden, gains[1], biases[1]).astype(jnp.bfloat16)
    return (normed, mixed, logsum, attended, hidden, second)


def front_back(block_in, saved, grad_top, grad_second, gains, biases, weight_qkv, weight_out):
    normed, mixed, logsum, attended, hidden = saved
    grad_mid, gain_two, bias_two = norm_back(hidden, gains[1], biases[1], grad_second)
    grad_hidden = grad_top + grad_mid
    grad_normed, grad_wqkv, grad_wout = attend_back(
        normed, mixed, logsum, attended, grad_hidden, weight_qkv, weight_out
    )
    grad_start, gain_one, bias_one = norm_back(
        block_in.astype(jnp.float32), gains[0], biases[0], grad_normed
    )
    return (
        grad_start + grad_hidden,
        grad_wqkv,
        grad_wout,
        jnp.stack([gain_one, gain_two]),
        jnp.stack([bias_one, bias_two]),
    )


def halve(array, axis, size, which):
    return lax.dynamic_slice_in_dim(array, which * size, size, axis)


def add_all(terms):
    total = terms[0]
    for value in terms[1:]:
        total = total + value
    return total


def on_device(
    tokens,
    cotangent,
    norm_gains,
    norm_biases,
    qkv_weight,
    out_weight,
    dense_in,
    dense_out,
    expert_in,
    expert_out,
    routes,
    gates,
):
    rows = IMG_MB * SEQ
    width = tokens.shape[1]
    hidden_units = dense_in.shape[1]
    experts = lax.axis_size("experts")
    capacity = 2 * rows // experts
    section = lax.axis_index("section")
    gains = norm_gains[0]
    biases = norm_biases[0]
    weight_qkv = qkv_weight[0]
    weight_out = out_weight[0]
    local_in = expert_in[0]
    local_back = expert_out[0]
    half_units = hidden_units // 2
    half_width = width // 2
    other = 1 - section

    def on_section(which, compute, *operands):

        def silent(*values):
            return jax.tree.map(jnp.zeros_like, compute(*values))

        return lax.cond(section == which, compute, silent, *operands)

    full_in, full_back = (
        lax.all_gather(local_in, "dp", axis=1, tiled=True),
        lax.all_gather(local_back, "dp", axis=0, tiled=True),
    )
    weight_in, weight_back = (full_in, full_back)

    def route(index):
        chosen = routes[index * rows : (index + 1) * rows]
        flat = jnp.concatenate([chosen[:, 0], chosen[:, 1]])
        table = (flat[:, None] == jnp.arange(experts, dtype=jnp.int32)[None, :]).astype(jnp.int32)
        place = jnp.sum(
            (jnp.cumsum(table, axis=0, dtype=jnp.int32) - table) * table, axis=1, dtype=jnp.int32
        )
        kept = place < capacity
        slot = jnp.where(kept, flat * capacity + place, experts * capacity)
        pair = gates[index * rows : (index + 1) * rows]
        return (slot, kept, jnp.concatenate([pair[:, 0], pair[:, 1]]))

    def place_rows(values, slot):
        filled = (
            jnp.zeros((experts * capacity, width), jnp.bfloat16).at[slot].set(values, mode="drop")
        )
        return filled.reshape(experts, capacity, width)

    def pick_rows(buffer, slot, kept, factor):
        flat_rows = buffer.reshape(experts * capacity, width)
        picked = (
            jnp.take(flat_rows, jnp.where(kept, slot, 0), axis=0).astype(jnp.float32)
            * factor[:, None]
        )
        return picked[:rows] + picked[rows:]

    def expert_forward(rows_in):
        before = matmul(rows_in, weight_in)
        active = jax.nn.gelu(before).astype(jnp.bfloat16)
        return (matmul(active, weight_back), before, active)

    def expert_backward(grad_rows, rows_in, before, active):
        grad_active = matmul_cols(grad_rows, weight_back)
        grad_back = matmul_rows(active, grad_rows)
        grad_before = gelu_back(before, grad_active).astype(jnp.bfloat16)
        grad_in = matmul_rows(grad_before, rows_in)
        grad_input = matmul_cols(grad_before, weight_in)
        return (grad_input, grad_in, grad_back)

    def forward_first(index):
        block_in = tokens[index * rows : (index + 1) * rows]
        normed, mixed, logsum, attended, hidden, second = front_half(
            block_in, gains, biases, weight_qkv, weight_out
        )
        active = jax.nn.gelu(matmul(second, dense_in)).astype(jnp.bfloat16)
        result = (hidden + matmul(active, dense_out)).astype(jnp.bfloat16)
        return (result, (normed, mixed, logsum, attended, hidden, second))

    def backward_first(index, grad_result, record):
        block_in = tokens[index * rows : (index + 1) * rows]
        second = record[5]
        before = matmul(second, dense_in)
        active = jax.nn.gelu(before).astype(jnp.bfloat16)
        grad_back = matmul_rows(active, grad_result)
        grad_before = gelu_back(before, matmul_cols(grad_result, dense_out)).astype(jnp.bfloat16)
        grad_in = matmul_rows(second, grad_before)
        grad_second = matmul_cols(grad_before, dense_in)
        grad_start, grad_wqkv, grad_wout, grad_gain, grad_bias = front_back(
            block_in,
            record[:5],
            grad_result.astype(jnp.float32),
            grad_second,
            gains,
            biases,
            weight_qkv,
            weight_out,
        )
        return (grad_start, (grad_wqkv, grad_wout, grad_gain, grad_bias), (grad_in, grad_back))

    def second_section(index, inbox):

        def front_part(block_in):
            normed, mixed, logsum, attended, hidden, second = front_half(
                block_in, gains, biases, weight_qkv, weight_out
            )
            slot, kept, gate_flat = route(index)
            outgoing = place_rows(jnp.concatenate([second, second]), slot)
            grad_top = cotangent[index * rows : (index + 1) * rows].astype(jnp.float32)
            grad_sent = (jnp.concatenate([grad_top, grad_top]) * gate_flat[:, None]).astype(
                jnp.bfloat16
            )
            return (
                (normed, mixed, logsum, attended, hidden),
                outgoing,
                place_rows(grad_sent, slot),
            )

        saved_front, outgoing, grad_box = on_section(1, front_part, inbox)
        arrived = lax.all_to_all(outgoing, "experts", split_axis=0, concat_axis=0, tiled=True)
        rows_in = arrived.reshape(-1, width)
        partial_out, before, active = on_section(1, expert_forward, rows_in)
        returned = partial_out.astype(jnp.bfloat16)
        back_home = lax.all_to_all(
            returned.reshape(experts, capacity, width),
            "experts",
            split_axis=0,
            concat_axis=0,
            tiled=True,
        )
        grad_arrived = lax.all_to_all(grad_box, "experts", split_axis=0, concat_axis=0, tiled=True)
        grad_rows = grad_arrived.reshape(-1, width)
        grad_input, grad_in, grad_back = on_section(
            1, expert_backward, grad_rows, rows_in, before, active
        )
        grad_home = lax.all_to_all(
            grad_input.astype(jnp.bfloat16).reshape(experts, capacity, width),
            "experts",
            split_axis=0,
            concat_axis=0,
            tiled=True,
        )

        def back_part(block_in, saved, home_rows, home_grads):
            hidden = saved[4]
            slot, kept, gate_flat = route(index)
            final = hidden + pick_rows(home_rows, slot, kept, jnp.where(kept, gate_flat, 0.0))
            grad_top = cotangent[index * rows : (index + 1) * rows].astype(jnp.float32)
            grad_second = pick_rows(home_grads, slot, kept, kept.astype(jnp.float32))
            grad_start, grad_wqkv, grad_wout, grad_gain, grad_bias = front_back(
                block_in, saved, grad_top, grad_second, gains, biases, weight_qkv, weight_out
            )
            return (
                final.astype(jnp.bfloat16),
                grad_start,
                (grad_wqkv, grad_wout, grad_gain, grad_bias),
            )

        final, grad_start, shared = on_section(
            1, back_part, inbox, saved_front, back_home, grad_home
        )
        return (final, grad_start, shared, (grad_in, grad_back))

    records = [None] * MB
    outputs = [None] * MB
    input_grads = [None] * MB
    shared_terms = []
    dense_terms = []
    expert_terms = []
    zero_rows = jnp.zeros((rows, width), jnp.bfloat16)
    inbox = zero_rows
    for tick in range(MB + 2):
        outbox = zero_rows
        if tick < MB:
            result, record = on_section(0, lambda tick=tick: forward_first(tick))
            records[tick] = record
            outputs[tick] = result
            outbox = result
        if tick >= 2:
            index = tick - 2
            grad_start, shared, dense_pair = on_section(
                0,
                lambda grad_now, record, index=index: backward_first(index, grad_now, record),
                inbox,
                records[index],
            )
            input_grads[index] = input_grads[index] + grad_start
            shared_terms.append(shared)
            dense_terms.append(dense_pair)
        if 1 <= tick <= MB:
            index = tick - 1
            final, grad_start, shared, expert_pair = second_section(index, inbox)
            outputs[index] = outputs[index] + final
            input_grads[index] = grad_start
            shared_terms.append(shared)
            expert_terms.append(expert_pair)
            outbox = outbox + grad_start.astype(jnp.bfloat16)
        if tick <= MB:
            inbox = swapped(outbox, "section", 0)
    grad_qkv_local = add_all([term[0] for term in shared_terms])
    grad_out_local = add_all([term[1] for term in shared_terms])
    grad_gains = add_all([term[2] for term in shared_terms])
    grad_biases = add_all([term[3] for term in shared_terms])
    grad_dense_in = add_all([term[0] for term in dense_terms])
    grad_dense_out = add_all([term[1] for term in dense_terms])
    grad_expert_in = add_all([term[0] for term in expert_terms])
    grad_expert_out = add_all([term[1] for term in expert_terms])
    norm_stack = jnp.concatenate([grad_gains.T, grad_biases.T], axis=1)
    summed = (
        lax.psum_scatter(grad_qkv_local, ("experts", "dp"), scatter_dimension=0, tiled=True),
        lax.psum_scatter(grad_out_local, ("experts", "dp"), scatter_dimension=0, tiled=True),
        lax.psum_scatter(norm_stack, ("experts", "dp"), scatter_dimension=0, tiled=True),
        lax.psum_scatter(grad_dense_in, ("experts", "dp"), scatter_dimension=0, tiled=True),
        lax.psum_scatter(grad_dense_out, ("experts", "dp"), scatter_dimension=0, tiled=True),
    )
    grad_qkv, grad_out, grad_norms, grad_din, grad_dout = (
        summed[0],
        summed[1],
        summed[2],
        summed[3],
        summed[4],
    )
    expert_sums = (
        lax.psum_scatter(
            grad_expert_in.astype(jnp.bfloat16), "dp", scatter_dimension=0, tiled=True
        ).astype(jnp.float32),
        lax.psum_scatter(
            grad_expert_out.astype(jnp.bfloat16), "dp", scatter_dimension=0, tiled=True
        ).astype(jnp.float32),
    )
    grad_ein, grad_eout = (expert_sums[0], expert_sums[1])
    grad_ein = grad_ein.T
    leaving = (
        halve(grad_din, 1, half_units, other),
        halve(grad_dout, 1, half_width, other),
        halve(grad_ein, 0, half_width, other),
        halve(grad_eout, 1, half_width, other),
    )
    staying = (
        halve(grad_din, 1, half_units, section),
        halve(grad_dout, 1, half_width, section),
        halve(grad_ein, 0, half_width, section),
        halve(grad_eout, 1, half_width, section),
    )
    packed = jnp.concatenate([piece.reshape(-1) for piece in leaving])
    landed = swapped(packed.astype(jnp.bfloat16), "section", 0).astype(packed.dtype)
    joined = []
    offset = 0
    for piece in staying:
        joined.append(piece + landed[offset : offset + piece.size].reshape(piece.shape))
        offset += piece.size
    all_outputs = jnp.concatenate(outputs, axis=0)
    all_grads = jnp.concatenate(input_grads, axis=0)
    return (
        all_outputs[None],
        all_grads[None],
        grad_qkv[None],
        grad_out[None],
        grad_norms[:, :2].T[None],
        grad_norms[:, 2:].T[None],
        joined[0],
        joined[1],
        joined[2][None],
        joined[3][None],
    )


def solution(mesh):
    placed = (
        P(("experts", "dp"), None),
        P(("experts", "dp"), None),
        P("section", None, None),
        P("section", None, None),
        P("section", None, None),
        P("section", None, None),
        P(),
        P(),
        P("experts", None, "dp"),
        P("experts", "dp", None),
        P(("experts", "dp"), None),
        P(("experts", "dp"), None),
    )
    return jax.shard_map(
        on_device,
        mesh=mesh,
        in_specs=placed,
        out_specs=(
            P("section", ("experts", "dp"), None),
            P("section", ("experts", "dp"), None),
            P("section", ("experts", "dp"), None),
            P("section", ("experts", "dp"), None),
            P("section", None, ("experts", "dp")),
            P("section", None, ("experts", "dp")),
            P(("experts", "dp"), "section"),
            P(("experts", "dp"), "section"),
            P("experts", "section", "dp"),
            P("experts", "dp", "section"),
        ),
        check_vma=False,
    )
```

profile of v0, /device:TPU:0, one launch (start us, length us, event | category | flops | bytes accessed | tf_op | source)
XLA Modules:
  0.0 1435.8 jit_solution(13558039832519068342)
XLA Ops:
  8.7 23.1 %conditional.12 = (bf16[197,768]{1,0:T(8,128)(2,1)S(1)}, bf16[197,768]{1,0:T(8,128)(2,1)S(1)}, bf16[197,2304]{1,0:T(8,128)(2,1)}, f32[1,12,197,1]{2,1,3,0:T(8,12...) conditional(s32[]{:T(128)} %convert_element_type.353, () %tuple.107, ...), branch_computations={%region_0.0_spmd, %region_1.0_spmd} | conditional | flops 2921466880 | bytes 40923912 | solution.py:185
  33.5 9.0 conditional.13
  42.5 17.6 %all_to_all.40 = bf16[4,98,768]{2,1,0:T(8,128)(2,1)} all-to-all(bf16[4,98,768]{2,1,0:T(8,128)(2,1)S(1)} %get-tuple-element.388), channel_id=1, replica_groups=mesh['section'=2,'experts'=4,'dp'=4] {'experts'}, dimensions={0} | all-to-all | bytes 1204224 | tf_op jit(solution)/shard_map/all_to_all | solution.py:281
  69.5 58.8 %all-gather.7.cloned.1.call-done = bf16[1,3072,768]{2,1,0:T(8,128)(2,1)} async-done(((bf16[1,768,768]{2,1,0:T(8,128)(2,1)}), bf16[1,3072,768]{2,1,0:T(8,128)(2,1)}) %all-gather.7.cloned.1.call-update) | async-done | bytes 4718608 | tf_op jit(solution)/shard_map/all_gather | solution.py:189
  138.4 9.4 conditional.15
  156.5 24.4 %conditional.17 = (bf16[197,768]{1,0:T(8,128)(2,1)S(1)}, bf16[197,768]{1,0:T(8,128)(2,1)S(1)}, bf16[197,2304]{1,0:T(8,128)(2,1)}, f32[1,12,197,1]{2,1,3,0:T(8,12...) conditional(s32[]{:T(128)} %convert_element_type.353, () %tuple.117, ...), branch_computations={%region_43.45_spmd, %region_44.52_spmd} | conditional | flops 2921466880 | bytes 31941512 | solution.py:185
  181.8 20.2 %conditional.16 = (bf16[197,768]{1,0:T(8,128)(2,1)}, f32[197,768]{1,0:T(8,128)}, f32[2,768]{1,0:T(2,128)S(1)}, f32[2,768]{1,0:T(2,128)S(1)}, bf16[197,768]{1,0:T...) conditional(s32[]{:T(128)} %convert_element_type.354, () %tuple.109, ...), branch_computations={%region_25.26_spmd, %region_26.44_spmd} | conditional | flops 2176078592 | bytes 113011168 | solution.py:185
  203.0 63.1 %collective-permute-start.1 = (bf16[197,768]{1,0:T(8,128)(2,1)S(1)}, bf16[197,768]{1,0:T(8,128)(2,1)S(1)}, u32[]{:S(2)}, u32[]{:S(2)}) collective-permute-start(bf16[197,768]{1,0:T(8,128)(2,1)S(1)} %add.560), channel_id=1, source_target_pairs={{0,16},{16,0},{1,17},{17,1},{2,18},{18,2},{3,19},{19,3},{4,20},{20... | collective-permute-start | bytes 907784 | tf_op jit(solution)/shard_map/ppermute | solution.py:23
  272.1 15.8 %all_to_all.41 = bf16[4,98,768]{2,1,0:T(8,128)(2,1)} all-to-all(bf16[4,98,768]{2,1,0:T(8,128)(2,1)} %get-tuple-element.402), channel_id=1, replica_groups=mesh['section'=2,'experts'=4,'dp'=4] {'experts'}, dimensions={0} | all-to-all | bytes 1204224 | tf_op jit(solution)/shard_map/all_to_all | solution.py:281
  302.9 10.1 conditional.20
  312.9 9.7 add_convert_fusion.4
  322.7 10.1 add_convert_fusion.5
  339.5 9.4 all-to-all-done.5
  353.1 11.5 all-to-all-done.7
  364.6 7.0 conditional.21
  373.5 99.7 %collective-permute-start.2 = (bf16[197,768]{1,0:T(8,128)(2,1)}, bf16[197,768]{1,0:T(8,128)(2,1)S(1)}, u32[]{:S(2)}, u32[]{:S(2)}) collective-permute-start(bf16[197,768]{1,0:T(8,128)(2,1)} %convert_element_type.359), channel_id=1, source_target_pairs={{0,16},{16,0},{1,17},{17,1},{2,18},{18,2},{3,19},{19,3},{4,20},{20... | collective-permute-start | bytes 907784 | tf_op jit(solution)/shard_map/ppermute | solution.py:23
  473.2 92.2 %conditional.22 = (f32[197,768]{1,0:T(8,128)}, f32[2,768]{1,0:T(2,128)S(1)}, f32[2,768]{1,0:T(2,128)S(1)}, f32[3072,768]{1,0:T(8,128)}, f32[768,2304]{1,0:T(8,12...) conditional(s32[]{:T(128)} %convert_element_type.353, () %tuple.126, (bf16[197,2304]{1,0:T(8,128)(2,1)}, ...), branch_computations={%region_86.88_spmd, %region_87.102_spmd} | conditional | flops 6838589440 | bytes 173429312 | solution.py:185
  533.8 8.0 copy.213
  541.8 7.5 fusion.121
  555.4 9.7 copy.217
  565.5 89.3 %conditional.23 = (f32[197,768]{1,0:T(8,128)S(1)}, f32[2,768]{1,0:T(2,128)S(1)}, f32[2,768]{1,0:T(2,128)S(1)}, f32[3072,768]{1,0:T(8,128)}, f32[768,2304]{1,0:T(...) conditional(s32[]{:T(128)} %convert_element_type.353, () %tuple.128, (bf16[197,2304]{1,0:T(8,128)(2,1)}, ...), branch_computations={%region_101.103_spmd, %region_102.117_spmd} | conditional | flops 6838589440 | bytes 180698528 | solution.py:185
  623.2 8.0 copy.219
  631.3 7.5 fusion.182
  644.8 9.7 copy.223
  654.8 11.4 add.579
  666.3 13.0 add.576
  687.0 13.7 add_add_fusion.16
  707.1 128.8 %reduce-scatter.16.cloned.1.call-done = f32[192,768]{1,0:T(8,128)} async-done(((f32[3072,768]{1,0:T(8,128)}), f32[192,768]{1,0:T(8,128)}) %reduce-scatter.16.cloned.1.call-update) | async-done | bytes 589840 | tf_op jit(solution)/shard_map/reduce_scatter | solution.py:375
  836.9 175.1 %reduce-scatter.14.cloned.1.call-done = f32[48,3072]{1,0:T(8,128)} async-done(((f32[768,3072]{1,0:T(8,128)}), f32[48,3072]{1,0:T(8,128)}) %reduce-scatter.14.cloned.1.call-update) | async-done | bytes 589840 | tf_op jit(solution)/shard_map/reduce_scatter | solution.py:374
  1023.7 115.6 %reduce-scatter.22.cloned.1.call-done = f32[48,4]{1,0:T(8,128)} async-done(((f32[768,4]{1,0:T(8,128)}), f32[48,4]{1,0:T(8,128)}) %reduce-scatter.22.cloned.1.call-update) | async-done | bytes 784
  1155.8 117.1 %reduce-scatter.12.cloned.1.call-done = f32[48,768]{1,0:T(8,128)} async-done(((f32[768,768]{1,0:T(8,128)}), f32[48,768]{1,0:T(8,128)}) %reduce-scatter.12.cloned.1.call-update) | async-done | bytes 147472 | tf_op jit(solution)/shard_map/reduce_scatter | solution.py:372
  1272.9 156.2 %reduce-scatter.10.cloned.1.call-done = f32[48,2304]{1,0:T(8,128)} async-done(((f32[768,2304]{1,0:T(8,128)}), f32[48,2304]{1,0:T(8,128)}) %reduce-scatter.10.cloned.1.call-update) | async-done | bytes 442384 | tf_op jit(solution)/shard_map/reduce_scatter | solution.py:371
  (336 shorter events, 336.2 us)
Async XLA Ops:
  7.2 62.4 %all-gather.5.cloned.1.call-start = ((), (), s32[]{:S(2)}) async-start(), calls=%async_computation.21 | async-start | bytes 5898240 | tf_op jit(solution)/shard_map/all_gather | solution.py:188
  7.9 120.4 %all-gather.7.cloned.1.call-start = ((), (), s32[]{:S(2)}) async-start(), calls=%async_computation.22 | async-start | bytes 5898240 | tf_op jit(solution)/shard_map/all_gather | solution.py:189
  8.7 24.8 %copy-start.75 = (s32[394,2]{0,1:T(2,128)S(1)}, s32[394,2]{0,1:T(2,128)}, u32[]{:S(2)}) copy-start(s32[394,2]{0,1:T(2,128)} %param.48) | copy-start | bytes 9460
  8.7 24.8 %copy-start.76 = (f32[394,2]{0,1:T(2,128)S(1)}, f32[394,2]{0,1:T(2,128)}, u32[]{:S(2)}) copy-start(f32[394,2]{0,1:T(2,128)} %param.49) | copy-start | bytes 9460
  31.8 1.7 collective-permute-start
  42.5 85.8 %copy-start.9 = (bf16[197,2304]{1,0:T(8,128)(2,1)}, bf16[197,2304]{1,0:T(8,128)(2,1)S(1)}, u32[]{:S(2)}) copy-start(bf16[197,2304]{1,0:T(8,128)(2,1)S(1)} %get-tuple-element.391) | copy-start | bytes 2723332
  60.2 73.6 %all-to-all-start.2 = ((bf16[4,98,768]{2,1,0:T(8,128)(2,1)}), bf16[4,98,768]{2,1,0:T(8,128)(2,1)S(1)}, u32[]{:S(2)}, u32[]{:S(2)}) async-start(bf16[4,98,768]{2,1,0:T(8,128)(2,1)} %get-tuple-element.393), calls=%async_computation.2 | async-start | bytes 1277952 | tf_op jit(solution)/shard_map/all_to_all | solution.py:292
  133.8 18.5 %all-to-all-start.1 = ((bf16[4,98,768]{2,1,0:T(8,128)(2,1)}), bf16[4,98,768]{2,1,0:T(8,128)(2,1)S(1)}, u32[]{:S(2)}, u32[]{:S(2)}) async-start(bf16[4,98,768]{2,1,0:T(8,128)(2,1)} %reshape.1146), calls=%async_computation.1 | async-start | bytes 1277952 | tf_op jit(solution)/shard_map/all_to_all | solution.py:285
  147.8 8.7 copy-start
  147.8 8.7 copy-start.3
  147.8 8.7 copy-start.62
  147.9 8.7 copy-start.70
  152.3 28.7 %all-to-all-start.3 = ((bf16[4,98,768]{2,1,0:T(8,128)(2,1)}), bf16[4,98,768]{2,1,0:T(8,128)(2,1)}, u32[]{:S(2)}, u32[]{:S(2)}) async-start(bf16[4,98,768]{2,1,0:T(8,128)(2,1)} %reshape.1147), calls=%async_computation.3 | async-start | bytes 1277952 | tf_op jit(solution)/shard_map/all_to_all | solution.py:297
  202.0 65.4 %copy-start.71 = (f32[2,768]{1,0:T(2,128)}, f32[2,768]{1,0:T(2,128)S(1)}, u32[]{:S(2)}) copy-start(f32[2,768]{1,0:T(2,128)S(1)} %get-tuple-element.442) | copy-start | bytes 18436
  202.0 65.4 %copy-start.73 = (f32[2,768]{1,0:T(2,128)}, f32[2,768]{1,0:T(2,128)S(1)}, u32[]{:S(2)}) copy-start(f32[2,768]{1,0:T(2,128)S(1)} %get-tuple-element.438) | copy-start | bytes 18436
  203.0 64.3 %collective-permute-start.1 = (bf16[197,768]{1,0:T(8,128)(2,1)S(1)}, bf16[197,768]{1,0:T(8,128)(2,1)S(1)}, u32[]{:S(2)}, u32[]{:S(2)}) collective-permute-start(bf16[197,768]{1,0:T(8,128)(2,1)S(1)} %add.560), channel_id=1, source_target_pairs={{0,16},{16,0},{1,17},{17,1},{2,18},{18,2},{3,19},{19,3},{4,20},{20... | collective-permute-start | bytes 907784 | tf_op jit(solution)/shard_map/ppermute | solution.py:23
  272.1 15.8 %copy-start.41 = (bf16[4,98,768]{2,1,0:T(8,128)(2,1)}, bf16[4,98,768]{2,1,0:T(8,128)(2,1)S(1)}, u32[]{:S(2)}) copy-start(bf16[4,98,768]{2,1,0:T(8,128)(2,1)S(1)} %get-tuple-element.407) | copy-start | bytes 1806340
  287.9 15.0 %all-to-all-start.6 = ((bf16[4,98,768]{2,1,0:T(8,128)(2,1)}), bf16[4,98,768]{2,1,0:T(8,128)(2,1)S(1)}, u32[]{:S(2)}, u32[]{:S(2)}) async-start(bf16[4,98,768]{2,1,0:T(8,128)(2,1)} %copy-done.41), calls=%async_computation.6 | async-start | bytes 1277952 | tf_op jit(solution)/shard_map/all_to_all | solution.py:292
  291.4 409.3 %reduce-scatter.20.cloned.1.call-start = ((), (), s32[]{:S(2)}) async-start(), calls=%async_computation.20 | async-start | bytes 5898240 | tf_op jit(solution)/shard_map/reduce_scatter | solution.py:388
  322.7 379.9 %reduce-scatter.18.cloned.1.call-start = ((), (), s32[]{:S(2)}) async-start(), calls=%async_computation.19 | async-start | bytes 5898240 | tf_op jit(solution)/shard_map/reduce_scatter | solution.py:385
  333.9 15.0 %all-to-all-start.5 = ((bf16[4,98,768]{2,1,0:T(8,128)(2,1)}), bf16[4,98,768]{2,1,0:T(8,128)(2,1)S(1)}, u32[]{:S(2)}, u32[]{:S(2)}) async-start(bf16[4,98,768]{2,1,0:T(8,128)(2,1)} %reshape.1149), calls=%async_computation.5 | async-start | bytes 1277952 | tf_op jit(solution)/shard_map/all_to_all | solution.py:285
  348.9 15.7 %all-to-all-start.7 = ((bf16[4,98,768]{2,1,0:T(8,128)(2,1)}), bf16[4,98,768]{2,1,0:T(8,128)(2,1)}, u32[]{:S(2)}, u32[]{:S(2)}) async-start(bf16[4,98,768]{2,1,0:T(8,128)(2,1)} %reshape.1150), calls=%async_computation.7 | async-start | bytes 1277952 | tf_op jit(solution)/shard_map/all_to_all | solution.py:297
  353.0 482.8 %reduce-scatter.16.cloned.1.call-start = ((), (), s32[]{:S(2)}) async-start(), calls=%async_computation.18 | async-start | bytes 10027008 | tf_op jit(solution)/shard_map/reduce_scatter | solution.py:375
  364.6 108.6 %copy-start.69 = (f32[1,12,197,1]{2,1,3,0:T(8,128)S(1)}, f32[1,12,197,1]{2,1,3,0:T(8,128)}, u32[]{:S(2)}) copy-start(f32[1,12,197,1]{2,1,3,0:T(8,128)} %get-tuple-element.416) | copy-start | bytes 28372
  373.5 192.0 %collective-permute-start.2 = (bf16[197,768]{1,0:T(8,128)(2,1)}, bf16[197,768]{1,0:T(8,128)(2,1)S(1)}, u32[]{:S(2)}, u32[]{:S(2)}) collective-permute-start(bf16[197,768]{1,0:T(8,128)(2,1)} %convert_element_type.359), channel_id=1, source_target_pairs={{0,16},{16,0},{1,17},{17,1},{2,18},{18,2},{3,19},{19,3},{4,20},{20... | collective-permute-start | bytes 907784 | tf_op jit(solution)/shard_map/ppermute | solution.py:23
  644.8 9.7 copy-start.42
  654.7 11.4 copy-start.43
  666.2 345.7 %reduce-scatter.14.cloned.1.call-start = ((), (), s32[]{:S(2)}) async-start(), calls=%async_computation.17 | async-start | bytes 10027008 | tf_op jit(solution)/shard_map/reduce_scatter | solution.py:374
  679.3 460.0 %reduce-scatter.22.cloned.1.call-start = ((), (), s32[]{:S(2)}) async-start(), calls=%async_computation.23 | async-start | bytes 417792
  681.0 591.9 %reduce-scatter.12.cloned.1.call-start = ((), (), s32[]{:S(2)}) async-start(), calls=%async_computation.16 | async-start | bytes 2506752 | tf_op jit(solution)/shard_map/reduce_scatter | solution.py:372
  687.0 742.1 %reduce-scatter.10.cloned.1.call-start = ((), (), s32[]{:S(2)}) async-start(), calls=%async_computation.15 | async-start | bytes 7520256 | tf_op jit(solution)/shard_map/reduce_scatter | solution.py:371
  1016.2 125.3 %collective-permute-start.3 = (bf16[737280]{0:T(1024)(128)(2,1)}, bf16[737280]{0:T(1024)(128)(2,1)}, u32[]{:S(2)}, u32[]{:S(2)}) collective-permute-start(bf16[737280]{0:T(1024)(128)(2,1)} %pad_maximum_fusion.14), channel_id=1, source_target_pairs={{0,16},{16,0},{1,17},{17,1},{2,18},{18,2},{3,19},{19,3},{4,20},{20... | collective-permute-start | bytes 4423688 | tf_op jit(solution)/shard_map/ppermute | solution.py:23
  (38 other events, 131.4 us)
Sparse Core Ops, SparseCore 0:
  9.8 59.6 all-gather.4
  71.4 56.9 all-gather.6
  322.8 98.4 reduce-scatter.19
  424.1 56.9 reduce-scatter.17
  666.3 169.4 reduce-scatter.15
  841.4 170.5 reduce-scatter.13
  1017.2 122.0 reduce-scatter.21
  1144.8 128.0 reduce-scatter.11
  1278.8 150.2 reduce-scatter.9
where the time goes:
time: 1450 us; the launch traced here: 1440 us
  waiting for transfers between devices  789 us (54%)
  starting transfers between devices  187 us (13%)
  matrix products  144 us (10%)
  local copies, waits for them, and re-layouts  136 us (9%)
  other arithmetic  111 us (8%)
  blocking collectives  33.4 us (2%)
  loops' own time  22 us (2%)
  between operations  14.6 us (1%)
    reduce_scatter x1, waiting for transfers between devices, on_device(): lax.psum_scatter(grad_dense_in, ('experts', 'dp'), scatter_dimension=0, t...  175 us
    ppermute x4, starting transfers between devices, swapped(): return lax.ppermute(block, axis, route)  163 us
    reduce_scatter x1, waiting for transfers between devices, on_device(): lax.psum_scatter(grad_qkv_local, ('experts', 'dp'), scatter_dimension=0,...  156 us
    reduce_scatter x1, waiting for transfers between devices, on_device(): lax.psum_scatter(grad_dense_out, ('experts', 'dp'), scatter_dimension=0,...  129 us
    reduce_scatter x1, waiting for transfers between devices, on_device(): lax.psum_scatter(grad_out_local, ('experts', 'dp'), scatter_dimension=0,...  117 us
    unnamed x10, waiting for transfers between devices  117 us
    all_gather x1, waiting for transfers between devices, on_device(): lax.all_gather(local_back, 'dp', axis=0, tiled=True)  58.8 us
    another operation x44, local copies, waits for them, and re-layouts  55.8 us
  transfers between devices with their start and end apart: 19, of which 13 were waited for; matrix products, arithmetic and copies ran while one was open for 25% of the time, Pallas kernels for 0%

commit v1 on v0

v1 whole, which is shorter than its diff:
```python
import jax
import jax.numpy as jnp
from jax import lax
from jax.sharding import PartitionSpec as P

HEADS = 12
HEAD_DIM = 64
SEQ = 197


eps = 1e-06


def pair(block):
    return lax.ppermute(block, "section", [(0, 1), (1, 0)])


def layer_norm(values, gain, bias):
    centred = values - jnp.mean(values, axis=-1, keepdims=True)
    spread = jnp.mean(centred * centred, axis=-1, keepdims=True)
    return centred * lax.rsqrt(spread + eps) * gain + bias


def norm_back(values, gain, bias, cotan):
    _, pull = jax.vjp(layer_norm, values, gain, bias)
    return pull(cotan)


def gelu_back(before, cotan):
    _, pull = jax.vjp(jax.nn.gelu, before)
    return pull(cotan)[0]


def matmul(left, right):
    return jnp.dot(left, right, preferred_element_type=jnp.float32)


def matmul_rows(left, right):
    return lax.dot_general(
        left, right, (((0,), (0,)), ((), ())), preferred_element_type=jnp.float32
    )


def matmul_cols(left, right):
    return lax.dot_general(
        left, right, (((1,), (1,)), ((), ())), preferred_element_type=jnp.float32
    )


def head_split(mixed):
    return mixed.reshape(-1, SEQ, 3, HEADS, HEAD_DIM)


def score_table(split):
    return jnp.einsum(
        "bqhd,bkhd->bhqk", split[:, :, 0], split[:, :, 1], preferred_element_type=jnp.float32
    ) * HEAD_DIM ** (-0.5)


def attend(normed, weight_qkv):
    mixed = matmul(normed, weight_qkv).astype(jnp.bfloat16)
    split = head_split(mixed)
    scores = score_table(split)
    top = jnp.max(scores, axis=-1, keepdims=True)
    logsum = top + jnp.log(jnp.sum(jnp.exp(scores - top), axis=-1, keepdims=True))
    probs = jnp.exp(scores - logsum).astype(jnp.bfloat16)
    attended = jnp.einsum(
        "bhqk,bkhd->bqhd", probs, split[:, :, 2], preferred_element_type=jnp.float32
    )
    return (mixed, logsum, attended.reshape(normed.shape[0], -1).astype(jnp.bfloat16))


def attend_back(normed, mixed, logsum, attended, grad_hidden, weight_qkv, weight_out):
    grad_cast = grad_hidden.astype(jnp.bfloat16)
    grad_wout = matmul_rows(attended, grad_cast).astype(jnp.bfloat16)
    grad_att = matmul_cols(grad_cast, weight_out).astype(jnp.bfloat16)
    split = head_split(mixed)
    probs_full = jnp.exp(score_table(split) - logsum)
    probs = probs_full.astype(jnp.bfloat16)
    grad_heads = grad_att.reshape(-1, SEQ, HEADS, HEAD_DIM)
    grad_probs = jnp.einsum(
        "bqhd,bkhd->bhqk", grad_heads, split[:, :, 2], preferred_element_type=jnp.float32
    )
    grad_value = jnp.einsum(
        "bhqk,bqhd->bkhd", probs, grad_heads, preferred_element_type=jnp.float32
    )
    inner = jnp.sum(probs_full * grad_probs, axis=-1, keepdims=True)
    grad_scores = (probs_full * (grad_probs - inner) * HEAD_DIM ** (-0.5)).astype(jnp.bfloat16)
    grad_query = jnp.einsum(
        "bhqk,bkhd->bqhd", grad_scores, split[:, :, 1], preferred_element_type=jnp.float32
    )
    grad_key = jnp.einsum(
        "bhqk,bqhd->bkhd", grad_scores, split[:, :, 0], preferred_element_type=jnp.float32
    )
    grad_mixed = (
        jnp.stack([grad_query, grad_key, grad_value], axis=2)
        .reshape(normed.shape[0], -1)
        .astype(jnp.bfloat16)
    )
    return (
        matmul_cols(grad_mixed, weight_qkv),
        matmul_rows(normed, grad_mixed).astype(jnp.bfloat16),
        grad_wout,
    )


def front_half(block_in, gains, biases, weight_qkv, weight_out):
    start = block_in.astype(jnp.float32)
    normed = layer_norm(start, gains[0], biases[0]).astype(jnp.bfloat16)
    mixed, logsum, attended = attend(normed, weight_qkv)
    hidden = start + matmul(attended, weight_out)
    second = layer_norm(hidden, gains[1], biases[1]).astype(jnp.bfloat16)
    return (normed, mixed, logsum, attended, hidden, second)


def front_back(block_in, saved, grad_top, grad_second, gains, biases, weight_qkv, weight_out):
    normed, mixed, logsum, attended, hidden = saved
    grad_mid, gain_two, bias_two = norm_back(hidden, gains[1], biases[1], grad_second)
    grad_hidden = grad_top + grad_mid
    grad_normed, grad_wqkv, grad_wout = attend_back(
        normed, mixed, logsum, attended, grad_hidden, weight_qkv, weight_out
    )
    grad_start, gain_one, bias_one = norm_back(
        block_in.astype(jnp.float32), gains[0], biases[0], grad_normed
    )
    return (
        grad_start + grad_hidden,
        grad_wqkv,
        grad_wout,
        jnp.stack([gain_one, gain_two, bias_one, bias_two], axis=1),
    )


def rounded(values):
    return lax.reduce_precision(values, exponent_bits=8, mantissa_bits=7).astype(jnp.bfloat16)


def on_device(
    tokens,
    cotangent,
    norm_gains,
    norm_biases,
    qkv_weight,
    out_weight,
    dense_in,
    dense_out,
    expert_in,
    expert_out,
    routes,
    gates,
):
    rows = SEQ
    width = tokens.shape[1]
    experts = lax.axis_size("experts")
    capacity = 2 * rows // experts
    slots = experts * capacity
    section = lax.axis_index("section")
    first = section == 0
    everyone = ("experts", "dp")

    def ordered(mine, other, axis):
        return jnp.concatenate(
            [jnp.where(first, mine, other), jnp.where(first, other, mine)], axis=axis
        )

    def kept_half(array, axis):
        low, high = jnp.split(array, 2, axis=axis)
        return jnp.where(first, low, high)

    def sent_half(array, axis):
        low, high = jnp.split(array, 2, axis=axis)
        return jnp.where(first, high, low)

    def pair_sum(array):
        landed = pair(sent_half(array, 1)).astype(jnp.float32)
        return (kept_half(array, 1).astype(jnp.float32) + landed).astype(jnp.bfloat16)

    def scattered(array, axes):
        return lax.psum_scatter(array, axes, scatter_dimension=0, tiled=True)

    def both(own):
        other = pair(own)
        return (jnp.where(first, own, other), jnp.where(first, other, own))

    qkv_zero, qkv_one = both(qkv_weight[0])
    norms_zero, norms_one = both(jnp.concatenate([norm_gains[0], norm_biases[0]], axis=0))
    out_zero, out_one = both(out_weight[0])
    part_in = lax.all_gather(kept_half(expert_in[0], 0), "dp", axis=1, tiled=True)
    part_back = lax.all_gather(kept_half(expert_out[0], 1), "dp", axis=0, tiled=True)
    weight_in = ordered(part_in, pair(part_in), 0)
    weight_back = ordered(part_back, pair(part_back), 1)

    def own_block(array):
        return lax.dynamic_slice_in_dim(array, section * rows, rows, 0)

    block_in = own_block(tokens)
    grad_top = own_block(cotangent).astype(jnp.float32)
    chosen = own_block(routes)
    gate_pair = own_block(gates)

    flat = jnp.concatenate([chosen[:, 0], chosen[:, 1]])
    table = (flat[:, None] == jnp.arange(experts, dtype=jnp.int32)[None, :]).astype(jnp.int32)
    place = jnp.sum(
        (jnp.cumsum(table, axis=0, dtype=jnp.int32) - table) * table, axis=1, dtype=jnp.int32
    )
    slot = jnp.where(place < capacity, flat * capacity + place, slots)
    gate_flat = jnp.concatenate([gate_pair[:, 0], gate_pair[:, 1]])
    spread = (jnp.arange(slots, dtype=jnp.int32)[:, None] == slot[None, :]).astype(jnp.bfloat16)

    normed0, mixed0, logsum0, attended0, hidden0, second0 = front_half(
        block_in, norms_zero[:2], norms_zero[2:], qkv_zero, out_zero
    )
    before0 = matmul(second0, dense_in)
    active0 = jax.nn.gelu(before0).astype(jnp.bfloat16)
    middle = rounded(hidden0 + matmul(active0, dense_out))

    normed1, mixed1, logsum1, attended1, hidden1, second1 = front_half(
        middle, norms_one[:2], norms_one[2:], qkv_one, out_one
    )
    doubled = jnp.concatenate([grad_top, grad_top]) * gate_flat[:, None]
    outgoing = jnp.concatenate(
        [
            matmul(spread[:, :rows] + spread[:, rows:], second1).astype(jnp.bfloat16),
            matmul(spread, doubled.astype(jnp.bfloat16)).astype(jnp.bfloat16),
        ],
        axis=1,
    )
    arrived = lax.all_to_all(
        outgoing.reshape(experts, capacity, 2 * width),
        "experts",
        split_axis=0,
        concat_axis=0,
        tiled=True,
    ).reshape(slots, 2 * width)
    rows_in = arrived[:, :width]
    grad_rows = arrived[:, width:]
    before1 = matmul(rows_in, weight_in)
    active1 = jax.nn.gelu(before1).astype(jnp.bfloat16)
    returned = matmul(active1, weight_back).astype(jnp.bfloat16)
    grad_before1 = gelu_back(before1, matmul_cols(grad_rows, weight_back)).astype(jnp.bfloat16)
    grad_arrived = matmul_cols(grad_before1, weight_in).astype(jnp.bfloat16)
    home = lax.all_to_all(
        jnp.concatenate([returned, grad_arrived], axis=1).reshape(experts, capacity, 2 * width),
        "experts",
        split_axis=0,
        concat_axis=0,
        tiled=True,
    ).reshape(slots, 2 * width)
    expert_in_sum = scattered(
        pair_sum(matmul_rows(grad_before1, rows_in).astype(jnp.bfloat16)), "dp"
    )
    expert_out_sum = scattered(
        pair_sum(matmul_rows(active1, grad_rows).astype(jnp.bfloat16)), "dp"
    )

    picked = matmul_rows(spread, home[:, :width]) * gate_flat[:, None]
    final = (hidden1 + (picked[:rows] + picked[rows:])).astype(jnp.bfloat16)
    grad_second1 = matmul_rows(spread[:, :rows] + spread[:, rows:], home[:, width:])
    grad_middle, grad_qkv1, grad_out1, grad_norm1 = front_back(
        middle,
        (normed1, mixed1, logsum1, attended1, hidden1),
        grad_top,
        grad_second1,
        norms_one[:2],
        norms_one[2:],
        qkv_one,
        out_one,
    )
    shared1 = scattered(
        jnp.concatenate([pair_sum(grad_qkv1), pair_sum(grad_out1)], axis=1), everyone
    )

    grad_result = rounded(grad_middle)
    dense_out_sum = scattered(
        pair_sum(matmul_rows(active0, grad_result).astype(jnp.bfloat16)), everyone
    )
    grad_before0 = gelu_back(before0, matmul_cols(grad_result, dense_out)).astype(jnp.bfloat16)
    dense_in_sum = scattered(
        pair_sum(matmul_rows(second0, grad_before0).astype(jnp.bfloat16)), everyone
    )
    grad_tokens, grad_qkv0, grad_out0, grad_norm0 = front_back(
        block_in,
        (normed0, mixed0, logsum0, attended0, hidden0),
        grad_result.astype(jnp.float32),
        matmul_cols(grad_before0, dense_in),
        norms_zero[:2],
        norms_zero[2:],
        qkv_zero,
        out_zero,
    )
    shared0 = scattered(
        jnp.concatenate([pair_sum(grad_qkv0), pair_sum(grad_out0)], axis=1), everyone
    )
    norm_sum = scattered(
        jnp.where(first, grad_norm0, grad_norm1)
        + pair(jnp.where(first, grad_norm1, grad_norm0)),
        everyone,
    )

    own_shared = jnp.where(first, shared0, shared1)
    other_shared = pair(jnp.where(first, shared1, shared0))
    cut = qkv_weight.shape[2] // 2
    qkv_sum = ordered(own_shared[:, :cut], other_shared[:, :cut], 1).astype(jnp.float32)
    out_sum = ordered(own_shared[:, cut:], other_shared[:, cut:], 1).astype(jnp.float32)
    acts = ordered(
        jnp.where(first, middle, final), pair(jnp.where(first, final, middle)), 0
    )
    act_grads = ordered(
        jnp.where(first, grad_tokens, grad_middle),
        pair(jnp.where(first, grad_middle, grad_tokens)),
        0,
    )
    return (
        acts[None],
        act_grads[None],
        qkv_sum[None],
        out_sum[None],
        norm_sum[:, :2].T[None],
        norm_sum[:, 2:].T[None],
        dense_in_sum.astype(jnp.float32),
        dense_out_sum.astype(jnp.float32),
        expert_in_sum.astype(jnp.float32).T[None],
        expert_out_sum.astype(jnp.float32)[None],
    )


def solution(mesh):
    placed = (
        P(("experts", "dp"), None),
        P(("experts", "dp"), None),
        P("section", None, None),
        P("section", None, None),
        P("section", None, None),
        P("section", None, None),
        P(),
        P(),
        P("experts", None, "dp"),
        P("experts", "dp", None),
        P(("experts", "dp"), None),
        P(("experts", "dp"), None),
    )
    return jax.shard_map(
        on_device,
        mesh=mesh,
        in_specs=placed,
        out_specs=(
            P("section", ("experts", "dp"), None),
            P("section", ("experts", "dp"), None),
            P("section", ("experts", "dp"), None),
            P("section", ("experts", "dp"), None),
            P("section", None, ("experts", "dp")),
            P("section", None, ("experts", "dp")),
            P(("experts", "dp"), "section"),
            P(("experts", "dp"), "section"),
            P("experts", "section", "dp"),
            P("experts", "dp", "section"),
        ),
        check_vma=False,
    )
```

time: 1450 us -> 1000 us (0.69)
  starting transfers between devices: 187 us -> 14 us
  local copies, waits for them, and re-layouts: 136 us -> 38.7 us
  other arithmetic: 111 us -> 55.8 us
  matrix products: 144 us -> 106 us
  blocking collectives: 33.4 us -> 0 us
  waiting for transfers between devices: 789 us -> 760 us
  loops' own time: 22 us -> 0 us
    ppermute x4 -> x17, starting transfers between devices: 163 us -> 3.53 us  [pair(): return lax.ppermute(block, 'section', [(0, 1), (1, 0)])]
    unnamed x10, waiting for transfers between devices: 117 us -> 57.6 us
    another operation x44 -> x9, local copies, waits for them, and re-layouts: 55.8 us -> 0.05 us  [the longest x8 0.03 us: front_back(): jnp.stack([gain_one, gain_two, bias_one, bias_two], axis=1)]
    add x11 -> x1, other arithmetic: 52.5 us -> 0.03 us  [on_device(): jnp.where(first, grad_norm0, grad_norm1)]
    cond x56 -> x0, local copies, waits for them, and re-layouts: 44 us -> none  [the longest x6 41.9 us: on_section(): return lax.cond(section == which, compute, silent, *operands)]
    all_to_all x2 -> x0, blocking collectives: 33.4 us -> none  [second_section(): lax.all_to_all(outgoing, 'experts', split_axis=0, concat_axis=0, tiled=True)]
    all_gather x2, waiting for transfers between devices: 62.6 us -> 34 us  [the longest x1 33 us: on_device(): lax.all_gather(kept_half(expert_in[0], 0), 'dp', axis=1, tiled=True)]
    all_to_all x6 -> x2, waiting for transfers between devices: 29.1 us -> 51.6 us  [the longest x1 29.3 us: on_device(): lax.all_to_all(outgoing.reshape(experts, capacity, 2 * width), 'experts',...]
  transfers between devices with their start and end apart: 19 -> 28, of which waited for: 13 -> 17; matrix products, arithmetic and copies ran while one was open for 25% -> 17% of each run, Pallas kernels for 0% -> 0%
where the time goes in v1:
time: 1000 us; the launch traced here: 989 us
  waiting for transfers between devices  760 us (76%)
  matrix products  106 us (11%)
  other arithmetic  55.8 us (6%)
  local copies, waits for them, and re-layouts  38.7 us (4%)
  between operations  15.5 us (2%)
  starting transfers between devices  14 us (1%)
    reduce_scatter x6, waiting for transfers between devices, scattered(): return lax.psum_scatter(array, axes, scatter_dimension=0, tiled=True)  599 us
    unnamed x10, waiting for transfers between devices  57.6 us
    all_gather x1, waiting for transfers between devices, on_device(): lax.all_gather(kept_half(expert_in[0], 0), 'dp', axis=1, tiled=True)  33 us
    all_to_all x1, waiting for transfers between devices, on_device(): lax.all_to_all(outgoing.reshape(experts, capacity, 2 * width), 'experts',...  29.3 us
    dot_general x10, matrix products, matmul_rows(): lax.dot_general(left, right, (((0,), (0,)), ((), ())), preferred_element_...  22.9 us
    dot_general x8, matrix products, matmul_cols(): lax.dot_general(left, right, (((1,), (1,)), ((), ())), preferred_element_...  22.9 us
    all_to_all x1, waiting for transfers between devices, on_device(): lax.all_to_all(jnp.concatenate([returned, grad_arrived], axis=1).reshape(...  22.4 us
  transfers between devices with their start and end apart: 28, of which 17 were waited for; matrix products, arithmetic and copies ran while one was open for 17% of the time, Pallas kernels for 0%

profile of v1, /device:TPU:0, one launch (start us, length us, event | category | flops | bytes accessed | tf_op | source)
XLA Modules:
  0.0 989.3 jit_solution(2538378738568135439)
XLA Ops:
  17.5 33.0 %all-gather.6.cloned.1.call-done = bf16[1,384,3072]{2,1,0:T(8,128)(2,1)} async-done(((bf16[1,384,768]{2,1,0:T(8,128)(2,1)}), bf16[1,384,3072]{2,1,0:T(8,128)(2,1)}) %all-gather.6.cloned.1.call-update) | async-done | bytes 2359312 | tf_op jit(solution)/shard_map/all_gather | solution.py:188
  50.6 3.1 convolution_convert_fusion.7
  64.9 4.2 convolution_convert_fusion.6
  83.9 4.9 all-to-all-start
  89.8 29.3 %all-to-all-done = bf16[4,98,1536]{2,1,0:T(8,128)(2,1)} async-done(((bf16[4,98,1536]{2,1,0:T(8,128)(2,1)}), bf16[4,98,1536]{2,1,0:T(8,128)(2,1)}, u32[]{:S(2)}, u32[]{:S(2)}) %all-to-all-start) | async-done | bytes 1204256 | tf_op jit(solution)/shard_map/all_to_all | solution.py:228
  126.7 3.8 broadcast_select_fusion.7
  130.5 2.9 fusion.41
  133.4 4.7 fusion.8
  144.2 4.3 all-to-all-start.1
  148.9 4.5 convolution_convert_fusion.3
  156.4 22.4 %all-to-all-done.1 = bf16[4,98,1536]{2,1,0:T(8,128)(2,1)} async-done(((bf16[4,98,1536]{2,1,0:T(8,128)(2,1)}), bf16[4,98,1536]{2,1,0:T(8,128)(2,1)}, u32[]{:S(2)}, u32[]{:S(2)}) %all-to-all-start.1) | async-done | bytes 1204256 | tf_op jit(solution)/shard_map/all_to_all | solution.py:242
  189.4 3.2 fusion.61
  192.6 3.0 fusion.116
  195.5 6.0 fusion.66
  201.6 6.0 fusion.63
  209.1 5.1 fusion.99
  225.7 3.0 fusion.114
  228.7 4.6 fusion.69
  233.4 4.6 fusion.72
  245.4 5.4 add_convert_fusion.1
  264.0 2.9 collective-permute-done.8
  269.6 5.4 convolution_convert_fusion.2
  275.6 4.4 collective-permute-done.16
  282.5 3.8 convolution_convert_fusion
  286.9 4.4 collective-permute-done.14
  309.1 57.5 %reduce-scatter.22.cloned.1.call-done = f32[48,4]{1,0:T(8,128)} async-done(((f32[768,4]{1,0:T(8,128)}), f32[48,4]{1,0:T(8,128)}) %reduce-scatter.22.cloned.1.call-update) | async-done | bytes 784
  372.5 33.5 %reduce-scatter.18.cloned.1.call-done = bf16[768,384]{1,0:T(8,128)(2,1)} async-done(((bf16[3072,384]{1,0:T(8,128)(2,1)}), bf16[768,384]{1,0:T(8,128)(2,1)}) %reduce-scatter.18.cloned.1.call-update) | async-done | bytes 589840 | tf_op jit(solution)/shard_map/reduce_scatter | solution.py:179
  408.5 131.7 %reduce-scatter.12.cloned.1.call-done = bf16[48,1536]{1,0:T(8,128)(2,1)} async-done(((bf16[768,1536]{1,0:T(8,128)(2,1)}), bf16[48,1536]{1,0:T(8,128)(2,1)}) %reduce-scatter.12.cloned.1.call-update) | async-done | bytes 147472 | tf_op jit(solution)/shard_map/reduce_scatter | solution.py:179
  540.2 133.3 %reduce-scatter.10.cloned.1.call-done = bf16[48,1536]{1,0:T(8,128)(2,1)} async-done(((bf16[768,1536]{1,0:T(8,128)(2,1)}), bf16[48,1536]{1,0:T(8,128)(2,1)}) %reduce-scatter.10.cloned.1.call-update) | async-done | bytes 147472 | tf_op jit(solution)/shard_map/reduce_scatter | solution.py:179
  674.7 38.3 %reduce-scatter.20.cloned.1.call-done = bf16[768,384]{1,0:T(8,128)(2,1)} async-done(((bf16[3072,384]{1,0:T(8,128)(2,1)}), bf16[768,384]{1,0:T(8,128)(2,1)}) %reduce-scatter.20.cloned.1.call-update) | async-done | bytes 589840 | tf_op jit(solution)/shard_map/reduce_scatter | solution.py:179
  716.7 130.7 %reduce-scatter.16.cloned.1.call-done = bf16[192,384]{1,0:T(8,128)(2,1)} async-done(((bf16[3072,384]{1,0:T(8,128)(2,1)}), bf16[192,384]{1,0:T(8,128)(2,1)}) %reduce-scatter.16.cloned.1.call-update) | async-done | bytes 147472 | tf_op jit(solution)/shard_map/reduce_scatter | solution.py:179
  849.0 131.7 %reduce-scatter.14.cloned.1.call-done = bf16[48,1536]{1,0:T(8,128)(2,1)} async-done(((bf16[768,1536]{1,0:T(8,128)(2,1)}), bf16[48,1536]{1,0:T(8,128)(2,1)}) %reduce-scatter.14.cloned.1.call-update) | async-done | bytes 147472 | tf_op jit(solution)/shard_map/reduce_scatter | solution.py:179
  (325 shorter events, 138.1 us)
Async XLA Ops:
  7.2 43.3 %all-gather.6.cloned.1.call-start = ((), (), s32[]{:S(2)}) async-start(), calls=%async_computation.16 | async-start | bytes 2949120 | tf_op jit(solution)/shard_map/all_gather | solution.py:188
  7.3 7.2 copy-start.53
  7.3 7.7 copy-start.15
  9.6 80.2 %all-gather.4.cloned.1.call-start = ((), (), s32[]{:S(2)}) async-start(), calls=%async_computation.9 | async-start | bytes 2949120 | tf_op jit(solution)/shard_map/all_gather | solution.py:189
  9.6 40.9 %collective-permute-start.1 = (bf16[768,2304]{1,0:T(8,128)(2,1)}, bf16[768,2304]{1,0:T(8,128)(2,1)}, u32[]{:S(2)}, u32[]{:S(2)}) collective-permute-start(bf16[768,2304]{1,0:T(8,128)(2,1)} %bitcast.240), channel_id=1, source_target_pairs={{0,16},{16,0},{1,17},{17,1},{2,18},{18,2},{3,19},{19,3},{4,20},{20... | collective-permute-start | bytes 10616840 | tf_op jit(solution)/shard_map/ppermute | solution.py:15
  10.9 6.5 collective-permute-start
  11.0 48.3 %collective-permute-start.2 = (bf16[768,768]{1,0:T(8,128)(2,1)}, bf16[768,768]{1,0:T(8,128)(2,1)}, u32[]{:S(2)}, u32[]{:S(2)}) collective-permute-start(bf16[768,768]{1,0:T(8,128)(2,1)} %bitcast.220), channel_id=1, source_target_pairs={{0,16},{16,0},{1,17},{17,1},{2,18},{18,2},{3,19},{19,3},{4,20},{20... | collective-permute-start | bytes 3538952 | tf_op jit(solution)/shard_map/ppermute | solution.py:15
  14.9 38.8 %copy-start.50 = (f32[197]{0:T(256)}, f32[197]{0:T(256)S(1)}, u32[]{:S(2)}) copy-start(f32[197]{0:T(256)S(1)} %fusion.96) | copy-start | bytes 2368
  50.5 71.2 %collective-permute-start.3 = (bf16[384,3072]{1,0:T(8,128)(2,1)}, bf16[384,3072]{1,0:T(8,128)(2,1)}, u32[]{:S(2)}, u32[]{:S(2)}) collective-permute-start(bf16[384,3072]{1,0:T(8,128)(2,1)} %bitcast.215), channel_id=1, source_target_pairs={{0,16},{16,0},{1,17},{17,1},{2,18},{18,2},{3,19},{19,3},{4,20},{20... | collective-permute-start | bytes 7077896 | tf_op jit(solution)/shard_map/ppermute | solution.py:15
  83.9 35.2 %all-to-all-start = ((bf16[4,98,1536]{2,1,0:T(8,128)(2,1)}), bf16[4,98,1536]{2,1,0:T(8,128)(2,1)}, u32[]{:S(2)}, u32[]{:S(2)}) async-start(bf16[4,98,1536]{2,1,0:T(8,128)(2,1)} %reshape.441), calls=%async_computation | async-start | bytes 2555904 | tf_op jit(solution)/shard_map/all_to_all | solution.py:228
  89.8 36.9 %collective-permute-start.4 = (bf16[3072,384]{1,0:T(8,128)(2,1)}, bf16[3072,384]{1,0:T(8,128)(2,1)}, u32[]{:S(2)}, u32[]{:S(2)}) collective-permute-start(bf16[3072,384]{1,0:T(8,128)(2,1)} %all-gather.4.cloned.1.call-done), channel_id=1, source_target_pairs={{0,16},{16,0},{1,17},{17,1},{2,18},{18,2},{3,19},{19,3},{4,20},{20... | collective-permute-start | bytes 7077896 | tf_op jit(solution)/shard_map/ppermute | solution.py:15
  144.2 34.6 %all-to-all-start.1 = ((bf16[4,98,1536]{2,1,0:T(8,128)(2,1)}), bf16[4,98,1536]{2,1,0:T(8,128)(2,1)}, u32[]{:S(2)}, u32[]{:S(2)}) async-start(bf16[4,98,1536]{2,1,0:T(8,128)(2,1)} %reshape.443), calls=%async_computation.1 | async-start | bytes 2555904 | tf_op jit(solution)/shard_map/all_to_all | solution.py:242
  148.5 218.1 %reduce-scatter.22.cloned.1.call-start = ((), (), s32[]{:S(2)}) async-start(), calls=%async_computation.17 | async-start | bytes 417792
  156.4 89.0 %collective-permute-start.15 = (bf16[3072,384]{1,0:T(8,128)(2,1)}, bf16[3072,384]{1,0:T(8,128)(2,1)}, u32[]{:S(2)}, u32[]{:S(2)}) collective-permute-start(bf16[3072,384]{1,0:T(8,128)(2,1)} %broadcast_select_fusion.4), channel_id=1, source_target_pairs={{0,16},{16,0},{1,17},{17,1},{2,18},{18,2},{3,19},{19,3},{4,20},{20... | collective-permute-start | bytes 7077896 | tf_op jit(solution)/shard_map/ppermute | solution.py:15
  243.1 1.2 collective-permute-start.12
  245.3 160.7 %reduce-scatter.18.cloned.1.call-start = ((), (), s32[]{:S(2)}) async-start(), calls=%async_computation.14 | async-start | bytes 2949120 | tf_op jit(solution)/shard_map/reduce_scatter | solution.py:179
  250.8 289.4 %reduce-scatter.12.cloned.1.call-start = ((), (), s32[]{:S(2)}) async-start(), calls=%async_computation.11 | async-start | bytes 2506752 | tf_op jit(solution)/shard_map/reduce_scatter | solution.py:179
  253.6 4.8 collective-permute-start.9
  255.4 2.8 collective-permute-start.10
  260.8 412.8 %reduce-scatter.10.cloned.1.call-start = ((), (), s32[]{:S(2)}) async-start(), calls=%async_computation.10 | async-start | bytes 2506752 | tf_op jit(solution)/shard_map/reduce_scatter | solution.py:179
  262.4 4.8 collective-permute-start.7
  263.8 3.2 collective-permute-start.8
  269.6 443.4 %reduce-scatter.20.cloned.1.call-start = ((), (), s32[]{:S(2)}) async-start(), calls=%async_computation.15 | async-start | bytes 2949120 | tf_op jit(solution)/shard_map/reduce_scatter | solution.py:179
  275.3 7.2 copy-start.3
  275.3 4.6 collective-permute-start.16
  282.2 565.1 %reduce-scatter.16.cloned.1.call-start = ((), (), s32[]{:S(2)}) async-start(), calls=%async_computation.13 | async-start | bytes 2506752 | tf_op jit(solution)/shard_map/reduce_scatter | solution.py:179
  286.6 4.6 collective-permute-start.14
  293.5 687.1 %reduce-scatter.14.cloned.1.call-start = ((), (), s32[]{:S(2)}) async-start(), calls=%async_computation.12 | async-start | bytes 2506752 | tf_op jit(solution)/shard_map/reduce_scatter | solution.py:179
  296.6 4.6 collective-permute-start.13
  307.1 61.7 %collective-permute-start.5 = (bf16[197,768]{1,0:T(8,128)(2,1)}, bf16[197,768]{1,0:T(8,128)(2,1)S(1)}, u32[]{:S(2)}, u32[]{:S(2)}) collective-permute-start(bf16[197,768]{1,0:T(8,128)(2,1)} %get-tuple-element.68), channel_id=1, source_target_pairs={{0,16},{16,0},{1,17},{17,1},{2,18},{18,2},{3,19},{19,3},{4,20},{20... | collective-permute-start | bytes 907784 | tf_op jit(solution)/shard_map/ppermute | solution.py:15
  308.8 61.0 %collective-permute-start.6 = (f32[197,768]{1,0:T(8,128)}, f32[197,768]{1,0:T(8,128)S(1)}, u32[]{:S(2)}, u32[]{:S(2)}) collective-permute-start(f32[197,768]{1,0:T(8,128)} %fusion.118), channel_id=1, source_target_pairs={{0,16},{16,0},{1,17},{17,1},{2,18},{18,2},{3,19},{19,3},{4,20},{20... | collective-permute-start | bytes 1815560 | tf_op jit(solution)/shard_map/ppermute | solution.py:15
  674.6 40.6 %collective-permute-start.11 = (bf16[48,1536]{1,0:T(8,128)(2,1)S(1)}, bf16[48,1536]{1,0:T(8,128)(2,1)S(1)}, u32[]{:S(2)}, u32[]{:S(2)}) collective-permute-start(bf16[48,1536]{1,0:T(8,128)(2,1)S(1)} %get-tuple-element.81), channel_id=1, source_target_pairs={{0,16},{16,0},{1,17},{17,1},{2,18},{18,2},{3,19},{19,3},{4,20},{20... | collective-permute-start | bytes 442376 | tf_op jit(solution)/shard_map/ppermute | solution.py:15
  (62 other events, 176.6 us)
Sparse Core Ops, SparseCore 0:
  10.4 40.0 all-gather.5
  52.4 37.3 all-gather.3
  245.4 121.0 reduce-scatter.21
  369.5 36.4 reduce-scatter.17
  410.8 129.4 reduce-scatter.11
  545.0 128.5 reduce-scatter.9
  676.6 36.3 reduce-scatter.19
  717.9 129.3 reduce-scatter.15
  852.2 128.3 reduce-scatter.13
